TPU v7x, 32 devices: a whole 2x2x4 slice. The times are simulated.
32 devices in a mesh: day: 2 (over y), stu: 16 (over z, x, core).
Axes of the slice: x: 2, y: 2, z: 4, core: 2. Of those that a mesh axis runs over, the one named last changes fastest.
Arguments:
- performance: bfloat16 [64, 128, 1024], P('day', 'stu'), may hold values from -8 to 8
- student_factor: bfloat16 [128, 256], P('stu'), may hold values from -0.5 to 0.5
- skill_factor: bfloat16 [1024, 256], replicated, may hold values from -0.1875 to 0.1875
- day_prev: float32 [64, 256], P('day'), may hold values from -6 to 6
- ar_coef: float32 [7], replicated, may hold values from -0.3 to 0.3
Outputs:
- day_factor: float32 [64, 256], P('day', 'stu')
- residual: float32 [64, 256], P('day', 'stu')
All inputs are finite; a program needn't handle non-finite values.
Results may differ from a plain program's by a relative error of at most 0.0003.
Values sent between devices are 32-bit elements; how exact they have to be, the bound alone decides.
No kernel may reach another device: no remote copies, remote signals or barrier semaphores. Data moves between devices by JAX's collectives and lax.ppermute only.
A program may use at most 64 MiB of HBM per device.

v0:
```python
import jax
import jax.numpy as jnp
from jax import lax
from jax.sharding import PartitionSpec as P

LAGS = 7
ITERS = 3
smoothing = 1.0


def shifted(block, axis, distance):
    devices = range(lax.axis_size(axis))
    route = [(i - distance, i) for i in devices if i - distance in devices]
    return lax.ppermute(block, axis, route)


def filter_rows(extended, coef, count):
    out = extended[LAGS : LAGS + count]
    for lag in range(1, LAGS + 1):
        out = out - coef[lag - 1] * extended[LAGS - lag : LAGS - lag + count]
    return out


def smooth(values, coef):
    count = values.shape[0]
    below = shifted(values[count - LAGS :], "day", 1)
    ahead_core = filter_rows(jnp.concatenate([below, values], 0), coef, count)
    above = shifted(ahead_core[:LAGS], "day", -1)
    ahead = jnp.concatenate([ahead_core, above], 0)
    out = ahead[:count]
    for lag in range(1, LAGS + 1):
        out = out - coef[lag - 1] * ahead[lag : lag + count]
    return out


def with_gram(values, gram_part):
    return jnp.dot(
        lax.all_gather(values, "stu", axis=1, tiled=True),
        gram_part,
        precision=lax.Precision.HIGHEST,
        preferred_element_type=jnp.float32,
    )


def operate(values, gram_part, coef):
    return with_gram(values, gram_part) + smoothing * smooth(values, coef)


def global_total(value):
    return lax.psum(value, ("day", "stu"))


def summed_gram(local_gram):
    return lax.psum(local_gram, "stu")


def local(performance, student_factor, skill_factor, day_prev, ar_coef):
    days, students, skills = performance.shape
    rank = skill_factor.shape[1]
    proj = jnp.dot(
        performance.reshape(days * students, skills),
        skill_factor,
        preferred_element_type=jnp.float32,
    )
    proj = proj.reshape(days, students, rank)
    local_terms = jnp.sum(proj * student_factor.astype(jnp.float32)[None], axis=1)
    local_gram = jnp.dot(student_factor.T, student_factor, preferred_element_type=jnp.float32)
    skill_gram = jnp.dot(skill_factor.T, skill_factor, preferred_element_type=jnp.float32)
    columns = rank // lax.axis_size("stu")
    first_col = lax.axis_index("stu") * columns
    gram = summed_gram(local_gram) * skill_gram
    mttkrp = lax.psum_scatter(local_terms, "stu", scatter_dimension=1, tiled=True)
    gram_part = lax.dynamic_slice_in_dim(gram, first_col, columns, 1)
    day_factor = lax.dynamic_slice_in_dim(day_prev, first_col, columns, 1)
    residual = mttkrp - operate(day_factor, gram_part, ar_coef)
    direction = residual
    norm_now = global_total(jnp.sum(residual * residual))
    for step in range(ITERS):
        image = operate(direction, gram_part, ar_coef)
        alpha = norm_now / global_total(jnp.sum(direction * image))
        day_factor = day_factor + alpha * direction
        residual = residual - alpha * image
        norm_next = global_total(jnp.sum(residual * residual))
        direction = residual + norm_next / norm_now * direction
        norm_now = norm_next
    return (day_factor, residual)


def solution(mesh):
    return jax.shard_map(
        local,
        mesh=mesh,
        in_specs=(P("day", "stu", None), P("stu", None), P(), P("day", None), P()),
        out_specs=(P("day", "stu"), P("day", "stu")),
        check_vma=False,
    )
```

profile of v0, /device:TPU:14, one launch (start us, length us, event | category | flops | bytes accessed | tf_op | source)
XLA Modules:
  0.0 491.8 jit_solution(908321572501885240)
XLA Ops:
  7.2 0.9 constant_dynamic-slice_fusion
  8.1 0.1 copy.10
  8.2 0.1 slice.333
  8.3 1.3 collective-permute-start
  9.6 1.7 fusion.139
  11.3 0.0 reduce-scatter.2.cloned.1.call-start
  11.3 0.6 copy-done.2
  11.9 0.3 fusion
  12.3 0.8 copy.9
  13.1 0.3 fusion.140
  13.4 0.3 copy-done.3
  13.7 0.7 fusion.138
  14.3 15.5 %all_gather.12 = f32[32,256]{0,1:T(8,128)S(1)} all-gather(f32[32,16]{0,1:T(8,128)S(1)} %copy.10), channel_id=1, replica_groups=mesh['day'=2,'stu'=16] {'stu'}, dimensions={1}, use_global_device_ids=true | all-gather | bytes 34816 | tf_op jit(solution)/shard_map/all_gather | solution.py:38
  29.8 4.5 fusion.120
  34.3 4.6 collective-permute-start.1
  38.9 64.2 %all-reduce.3.cloned.1.call-done = f32[256,256]{0,1:T(8,128)} async-done(((f32[256,256]{0,1:T(8,128)}), f32[256,256]{0,1:T(8,128)}) %all-reduce.3.cloned.1.call-update) | async-done | bytes 262160 | tf_op jit(solution)/shard_map/psum | solution.py:54
  103.1 0.7 dynamic-slice_multiply_fusion
  103.8 57.7 %reduce-scatter.2.cloned.1.call-done = f32[32,16]{0,1:T(8,128)} async-done(((f32[32,256]{0,1:T(8,128)}), f32[32,16]{0,1:T(8,128)}) %reduce-scatter.2.cloned.1.call-update) | async-done | bytes 2064 | tf_op jit(solution)/shard_map/reduce_scatter | solution.py:72
  161.5 5.2 %fusion.104 = f32[32,16]{0,1:T(8,128)S(1)} fusion(f32[32,16]{0,1:T(8,128)} %reduce-scatter.2.cloned.1.call-done, f32[7,16]{0,1:T(8,128)S(1)} %collective-permute-done.1, f32[32,16]{0,1:T(8,128)S(1)} %fusion.120, f32[]{:T(128)} %bitcast.7, f32[]{:T(128)} %bitcast.6, f32[]{:T(128)} %bitcast.5, f32[]{:T(128)} %bitcast.4, f32[]{:T(128)} %bitcast.3, ...), kind=kOutput, calls=%fused_computation.173 | convolution fusion | flops 1584640 | bytes 55772 | tf_op jit(solution)/shard_map/dot_general | solution.py:37
  166.7 0.1 slice.359
  166.8 1.3 collective-permute-start.2
  168.1 4.2 collective-permute-done.2
  172.3 4.5 fusion.86
  176.8 1.6 collective-permute-start.3
  178.5 15.4 %all_gather.13 = f32[32,256]{0,1:T(8,128)S(1)} all-gather(f32[32,16]{0,1:T(8,128)S(1)} %fusion.104), channel_id=1, replica_groups=mesh['day'=2,'stu'=16] {'stu'}, dimensions={1}, use_global_device_ids=true | all-gather | bytes 34816 | tf_op jit(solution)/shard_map/all_gather | solution.py:38
  193.8 5.2 %multiply_reduce_fusion.4 = (f32[]{:T(128)}, f32[]{:T(128)}, f32[32,16]{0,1:T(8,128)S(1)}) fusion(f32[32,16]{0,1:T(8,128)S(1)} %fusion.104, f32[7,16]{0,1:T(8,128)S(1)} %collective-permute-done.3, f32[32,16]{0,1:T(8,128)S(1)} %fusion.86, f32[]{:T(128)} %bitcast.7, f32[]{:T(128)} %bitcast.6, f32[]{:T(128)} %bitcast.5, f32[]{:T(128)} %bitcast.4, ...), kind=kOutput, calls=%fused_computation.235 | convolution fusion | flops 1586174 | bytes 55780 | tf_op jit(solution)/shard_map/dot_general | solution.py:37
  199.0 44.1 %all-reduce = (f32[]{:T(128)}, f32[]{:T(128)}) all-reduce(f32[]{:T(128)} %get-tuple-element.3, f32[]{:T(128)} %get-tuple-element.2), channel_id=1, replica_groups=mesh['day'=2,'stu'=16] {'day','stu'}, use_global_device_ids=true, to_apply=%region_4.0 | all-reduce | flops 2 | bytes 16 | tf_op jit(solution)/shard_map/psum | solution.py:50
  244.4 0.6 multiply_reduce_fusion.3
  245.1 38.6 %psum.52 = f32[]{:T(128)} all-reduce(f32[]{:T(128)} %multiply_reduce_fusion.3), channel_id=1, replica_groups=mesh['day'=2,'stu'=16] {'day','stu'}, use_global_device_ids=true, to_apply=%region_8.0 | all-reduce | flops 1 | bytes 8 | tf_op jit(solution)/shard_map/psum | solution.py:50
  285.1 0.1 slice.385
  285.1 1.3 collective-permute-start.4
  286.4 4.2 collective-permute-done.4
  290.7 4.5 fusion.53
  295.1 1.6 collective-permute-start.5
  296.8 18.0 %all_gather.14 = f32[32,256]{0,1:T(8,128)S(1)} all-gather(f32[32,16]{0,1:T(8,128)S(1)} %multiply_add_fusion.2), channel_id=1, replica_groups=mesh['day'=2,'stu'=16] {'stu'}, dimensions={1}, use_global_device_ids=true | all-gather | bytes 34816 | tf_op jit(solution)/shard_map/all_gather | solution.py:38
  314.8 5.2 %multiply_reduce_fusion.2 = (f32[]{:T(128)}, f32[32,16]{0,1:T(8,128)S(1)}) fusion(f32[32,16]{0,1:T(8,128)S(1)} %multiply_add_fusion.2, f32[7,16]{0,1:T(8,128)S(1)} %collective-permute-done.5, f32[32,16]{0,1:T(8,128)S(1)} %fusion.53, f32[]{:T(128)} %bitcast.7, f32[]{:T(128)} %bitcast.6, f32[]{:T(128)} %bitcast.5, f32[]{:T(128)} %bitcast.4, f32[]{:T(128)} %bitcast.3, ...), kind=kOutput, calls=%fused_computation.231 | convolution fusion | flops 1585151 | bytes 55776 | tf_op jit(solution)/shard_map/dot_general | solution.py:37
  320.0 43.0 %psum.53 = f32[]{:T(128)} all-reduce(f32[]{:T(128)} %get-tuple-element.10), channel_id=1, replica_groups=mesh['day'=2,'stu'=16] {'day','stu'}, use_global_device_ids=true, to_apply=%region_10.0 | all-reduce | flops 1 | bytes 8 | tf_op jit(solution)/shard_map/psum | solution.py:50
  364.2 0.6 multiply_reduce_fusion.1
  364.8 39.0 %psum.54 = f32[]{:T(128)} all-reduce(f32[]{:T(128)} %get-tuple-element.8), channel_id=1, replica_groups=mesh['day'=2,'stu'=16] {'day','stu'}, use_global_device_ids=true, to_apply=%region_12.0 | all-reduce | flops 1 | bytes 8 | tf_op jit(solution)/shard_map/psum | solution.py:50
  405.2 0.1 slice.411
  405.3 1.3 collective-permute-start.6
  406.5 4.2 collective-permute-done.6
  410.8 4.5 fusion.20
  415.3 1.6 collective-permute-start.7
  416.9 17.6 %all_gather.15 = f32[32,256]{0,1:T(8,128)S(1)} all-gather(f32[32,16]{0,1:T(8,128)S(1)} %multiply_add_fusion.1), channel_id=1, replica_groups=mesh['day'=2,'stu'=16] {'stu'}, dimensions={1}, use_global_device_ids=true | all-gather | bytes 34816 | tf_op jit(solution)/shard_map/all_gather | solution.py:38
  434.5 5.1 %multiply_reduce_fusion = (f32[]{:T(128)}, f32[32,16]{0,1:T(8,128)S(1)}) fusion(f32[32,16]{0,1:T(8,128)S(1)} %multiply_add_fusion.1, f32[7,16]{0,1:T(8,128)S(1)} %collective-permute-done.7, f32[32,16]{0,1:T(8,128)S(1)} %fusion.20, f32[]{:T(128)} %bitcast.7, f32[]{:T(128)} %bitcast.6, f32[]{:T(128)} %bitcast.5, f32[]{:T(128)} %bitcast.4, f32[]{:T(128)} %bitcast.3, ...), kind=kOutput, calls=%fused_computation.227 | convolution fusion | flops 1585151 | bytes 55776 | tf_op jit(solution)/shard_map/dot_general | solution.py:37
  439.7 43.2 %psum.55 = f32[]{:T(128)} all-reduce(f32[]{:T(128)} %get-tuple-element.6), channel_id=1, replica_groups=mesh['day'=2,'stu'=16] {'day','stu'}, use_global_device_ids=true, to_apply=%region_14.0 | all-reduce | flops 1 | bytes 8 | tf_op jit(solution)/shard_map/psum | solution.py:50
  484.3 0.6 multiply_subtract_fusion
  (17 shorter events, 0.1 us)
Async XLA Ops:
  7.2 4.8 copy-start
  7.2 4.8 copy-start.1
  7.2 95.9 %all-reduce.3.cloned.1.call-start = ((), (), s32[]{:S(2)}) async-start(), calls=%async_computation.2 | async-start | bytes 524288 | tf_op jit(solution)/shard_map/psum | solution.py:54
  8.3 21.6 %collective-permute-start = (f32[7,16]{0,1:T(8,128)S(1)}, f32[7,16]{0,1:T(8,128)S(1)}, u32[]{:S(2)}, u32[]{:S(2)}) collective-permute-start(f32[7,16]{0,1:T(8,128)S(1)} %slice.333), channel_id=1, source_target_pairs={{0,16},{1,17},{2,18},{3,19},{4,20},{5,21},{6,22},{7,23},{8,24},{9,... | collective-permute-start | bytes 1352 | tf_op jit(solution)/shard_map/ppermute | solution.py:14
  11.2 0.7 copy-start.2
  11.3 150.2 %reduce-scatter.2.cloned.1.call-start = ((), (), s32[]{:S(2)}) async-start(), calls=%async_computation.1 | async-start | bytes 139264 | tf_op jit(solution)/shard_map/reduce_scatter | solution.py:72
  13.0 0.7 copy-start.3
  34.3 69.5 %collective-permute-start.1 = (f32[7,16]{0,1:T(8,128)S(1)}, f32[7,16]{0,1:T(8,128)S(1)}, u32[]{:S(2)}, u32[]{:S(2)}) collective-permute-start(f32[7,16]{0,1:T(8,128)S(1)} %bitcast.27), channel_id=1, source_target_pairs={{16,0},{17,1},{18,2},{19,3},{20,4},{21,5},{22,6},{23,7},{24,8},{25... | collective-permute-start | bytes 1352 | tf_op jit(solution)/shard_map/ppermute | solution.py:14
  166.8 5.5 %collective-permute-start.2 = (f32[7,16]{0,1:T(8,128)S(1)}, f32[7,16]{0,1:T(8,128)S(1)}, u32[]{:S(2)}, u32[]{:S(2)}) collective-permute-start(f32[7,16]{0,1:T(8,128)S(1)} %slice.359), channel_id=1, source_target_pairs={{0,16},{1,17},{2,18},{3,19},{4,20},{5,21},{6,22},{7,23},{8,24},{9,... | collective-permute-start | bytes 1352 | tf_op jit(solution)/shard_map/ppermute | solution.py:14
  176.8 17.0 %collective-permute-start.3 = (f32[7,16]{0,1:T(8,128)S(1)}, f32[7,16]{0,1:T(8,128)S(1)}, u32[]{:S(2)}, u32[]{:S(2)}) collective-permute-start(f32[7,16]{0,1:T(8,128)S(1)} %bitcast.29), channel_id=1, source_target_pairs={{16,0},{17,1},{18,2},{19,3},{20,4},{21,5},{22,6},{23,7},{24,8},{25... | collective-permute-start | bytes 1352 | tf_op jit(solution)/shard_map/ppermute | solution.py:14
  285.1 5.5 %collective-permute-start.4 = (f32[7,16]{0,1:T(8,128)S(1)}, f32[7,16]{0,1:T(8,128)S(1)}, u32[]{:S(2)}, u32[]{:S(2)}) collective-permute-start(f32[7,16]{0,1:T(8,128)S(1)} %slice.385), channel_id=1, source_target_pairs={{0,16},{1,17},{2,18},{3,19},{4,20},{5,21},{6,22},{7,23},{8,24},{9,... | collective-permute-start | bytes 1352 | tf_op jit(solution)/shard_map/ppermute | solution.py:14
  295.1 19.6 %collective-permute-start.5 = (f32[7,16]{0,1:T(8,128)S(1)}, f32[7,16]{0,1:T(8,128)S(1)}, u32[]{:S(2)}, u32[]{:S(2)}) collective-permute-start(f32[7,16]{0,1:T(8,128)S(1)} %bitcast.30), channel_id=1, source_target_pairs={{16,0},{17,1},{18,2},{19,3},{20,4},{21,5},{22,6},{23,7},{24,8},{25... | collective-permute-start | bytes 1352 | tf_op jit(solution)/shard_map/ppermute | solution.py:14
  405.3 5.5 %collective-permute-start.6 = (f32[7,16]{0,1:T(8,128)S(1)}, f32[7,16]{0,1:T(8,128)S(1)}, u32[]{:S(2)}, u32[]{:S(2)}) collective-permute-start(f32[7,16]{0,1:T(8,128)S(1)} %slice.411), channel_id=1, source_target_pairs={{0,16},{1,17},{2,18},{3,19},{4,20},{5,21},{6,22},{7,23},{8,24},{9,... | collective-permute-start | bytes 1352 | tf_op jit(solution)/shard_map/ppermute | solution.py:14
  415.3 19.3 %collective-permute-start.7 = (f32[7,16]{0,1:T(8,128)S(1)}, f32[7,16]{0,1:T(8,128)S(1)}, u32[]{:S(2)}, u32[]{:S(2)}) collective-permute-start(f32[7,16]{0,1:T(8,128)S(1)} %bitcast.28), channel_id=1, source_target_pairs={{16,0},{17,1},{18,2},{19,3},{20,4},{21,5},{22,6},{23,7},{24,8},{25... | collective-permute-start | bytes 1352 | tf_op jit(solution)/shard_map/ppermute | solution.py:14
Sparse Core Ops, SparseCore 0:
  11.4 91.6 all-reduce.2
  106.5 54.8 reduce-scatter.1
where the time goes:
time: 494 us; the launch traced here: 492 us
  blocking collectives  274 us (55%)
  waiting for transfers between devices  135 us (27%)
  matrix products  23.1 us (5%)
  between operations  20.9 us (4%)
  other arithmetic  20.4 us (4%)
  starting transfers between devices  14.7 us (3%)
    psum x5, blocking collectives, global_total(): return lax.psum(value, ('day', 'stu'))  208 us
    all_gather x4, blocking collectives, with_gram(): lax.all_gather(values, 'stu', axis=1, tiled=True)  66.5 us
    psum x1, waiting for transfers between devices, summed_gram(): return lax.psum(local_gram, 'stu')  64.2 us
    reduce_scatter x1, waiting for transfers between devices, local(): lax.psum_scatter(local_terms, 'stu', scatter_dimension=1, tiled=True)  57.7 us
    dot_general x4, matrix products, with_gram(): jnp.dot(lax.all_gather(values, 'stu', axis=1, tiled=True), gram_part, pre...  20.8 us
    sub x4, other arithmetic, filter_rows(): out = out - coef[lag - 1] * extended[LAGS - lag:LAGS - lag + count]  17.8 us
    ppermute x8, starting transfers between devices, shifted(): return lax.ppermute(block, axis, route)  14.6 us
    ppermute x8, waiting for transfers between devices, shifted(): return lax.ppermute(block, axis, route)  12.7 us
  transfers between devices with their start and end apart: 10, of which 5 were waited for; matrix products, arithmetic and copies ran while one was open for 2% of the time, Pallas kernels for 0%

commit v1 on v0

--- a/solution.py
+++ b/solution.py
@@ -6,6 +6,17 @@
 LAGS = 7
 ITERS = 3
 smoothing = 1.0
+
+
+def gather_around(x, axis, dim):
+    ways = lax.axis_size(axis)
+    pieces = [x]
+    for far in range(1, ways):
+        pieces.append(
+            lax.ppermute(pieces[far - 1], axis, [(d, (d - 1) % ways) for d in range(ways)])
+        )
+    line = jnp.concatenate(pieces, axis=dim)
+    return jnp.roll(line, lax.axis_index(axis) * x.shape[dim], axis=dim)
 
 
 def shifted(block, axis, distance):
@@ -35,7 +46,7 @@
 
 def with_gram(values, gram_part):
     return jnp.dot(
-        lax.all_gather(values, "stu", axis=1, tiled=True),
+        gather_around(values, "stu", 1),
         gram_part,
         precision=lax.Precision.HIGHEST,
         preferred_element_type=jnp.float32,

time: 494 us -> 729 us (1.48)
  waiting for transfers between devices: 135 us -> 269 us
  starting transfers between devices: 14.7 us -> 114 us
    ppermute x0 -> x60, waiting for transfers between devices: none -> 132 us  [gather_around(): lax.ppermute(pieces[far - 1], axis, [(d, (d - 1) % ways) for d in range(w...]
    ppermute x0 -> x60, starting transfers between devices: none -> 91.4 us  [gather_around(): lax.ppermute(pieces[far - 1], axis, [(d, (d - 1) % ways) for d in range(w...]
    all_gather x4 -> x0, blocking collectives: 66.5 us -> none  [with_gram(): lax.all_gather(values, 'stu', axis=1, tiled=True)]
    psum x5, blocking collectives: 208 us -> 271 us  [global_total(): return lax.psum(value, ('day', 'stu'))]
    psum x1, waiting for transfers between devices: 64.2 us -> 78.9 us  [summed_gram(): return lax.psum(local_gram, 'stu')]
    ppermute x8, waiting for transfers between devices: 12.7 us -> 0.25 us  [shifted(): return lax.ppermute(block, axis, route)]
    ppermute x8, starting transfers between devices: 14.6 us -> 22.2 us  [shifted(): return lax.ppermute(block, axis, route)]
  transfers between devices with their start and end apart: 10 -> 70, of which waited for: 5 -> 58; matrix products, arithmetic and copies ran while one was open for 2% -> 4% of each run, Pallas kernels for 0% -> 0%
where the time goes in v1:
time: 729 us; the launch traced here: 725 us
  blocking collectives  271 us (37%)
  waiting for transfers between devices  269 us (37%)
  starting transfers between devices  114 us (16%)
  matrix products  22.8 us (3%)
  between operations  20.9 us (3%)
  other arithmetic  20.6 us (3%)
  local copies, waits for them, and re-layouts  7.9 us (1%)
    psum x5, blocking collectives, global_total(): return lax.psum(value, ('day', 'stu'))  271 us
    ppermute x60, waiting for transfers between devices, gather_around(): lax.ppermute(pieces[far - 1], axis, [(d, (d - 1) % ways) for d in range(w...  132 us
    ppermute x60, starting transfers between devices, gather_around(): lax.ppermute(pieces[far - 1], axis, [(d, (d - 1) % ways) for d in range(w...  91.4 us
    psum x1, waiting for transfers between devices, summed_gram(): return lax.psum(local_gram, 'stu')  78.9 us
    reduce_scatter x1, waiting for transfers between devices, local(): lax.psum_scatter(local_terms, 'stu', scatter_dimension=1, tiled=True)  57.7 us
    ppermute x8, starting transfers between devices, shifted(): return lax.ppermute(block, axis, route)  22.2 us
    dot_general x4, matrix products, with_gram(): jnp.dot(gather_around(values, 'stu', 1), gram_part, precision=lax.Precisi...  21.2 us
    sub x4, other arithmetic, filter_rows(): out = out - coef[lag - 1] * extended[LAGS - lag:LAGS - lag + count]  18 us
  transfers between devices with their start and end apart: 70, of which 58 were waited for; matrix products, arithmetic and copies ran while one was open for 4% of the time, Pallas kernels for 0%

profile of v1, /device:TPU:14, one launch (start us, length us, event | category | flops | bytes accessed | tf_op | source)
XLA Modules:
  0.0 725.5 jit_solution(4541474678584806756)
XLA Ops:
  20.6 4.0 collective-permute-done.4
  24.6 4.0 collective-permute-done.5
  28.6 4.0 collective-permute-done.6
  32.5 4.0 collective-permute-done.7
  36.5 4.0 collective-permute-done.8
  52.4 4.7 collective-permute-start.12
  58.5 3.8 collective-permute-start.13
  63.6 5.0 collective-permute-start.14
  68.7 4.5 fusion.142
  73.2 4.3 collective-permute-start.16
  78.7 78.9 %all-reduce.3.cloned.1.call-done = f32[256,256]{0,1:T(8,128)} async-done(((f32[256,256]{0,1:T(8,128)}), f32[256,256]{0,1:T(8,128)}) %all-reduce.3.cloned.1.call-update) | async-done | bytes 262160 | tf_op jit(solution)/shard_map/psum | solution.py:65
  158.3 57.7 %reduce-scatter.2.cloned.1.call-done = f32[32,16]{0,1:T(8,128)} async-done(((f32[32,256]{0,1:T(8,128)}), f32[32,16]{0,1:T(8,128)}) %reduce-scatter.2.cloned.1.call-update) | async-done | bytes 2064 | tf_op jit(solution)/shard_map/reduce_scatter | solution.py:83
  216.0 5.3 fusion.26
  236.8 3.2 collective-permute-done.22
  240.2 3.8 collective-permute-done.23
  244.2 3.8 collective-permute-done.24
  248.1 3.8 collective-permute-done.25
  252.1 3.8 collective-permute-done.26
  256.1 3.8 collective-permute-done.27
  260.1 3.8 collective-permute-done.28
  267.9 3.6 collective-permute-start.30
  272.9 4.9 collective-permute-start.31
  277.8 4.5 fusion.110
  282.3 4.3 collective-permute-start.33
  288.0 5.3 multiply_reduce_fusion.4
  293.3 62.6 %all-reduce = (f32[]{:T(128)}, f32[]{:T(128)}) all-reduce(f32[]{:T(128)} %get-tuple-element.4, f32[]{:T(128)} %get-tuple-element.3), channel_id=1, replica_groups=mesh['day'=2,'stu'=16] {'day','stu'}, use_global_device_ids=true, to_apply=%region_4.6 | all-reduce | flops 2 | bytes 16 | tf_op jit(solution)/shard_map/psum | solution.py:61
  357.7 40.3 %psum.52 = f32[]{:T(128)} all-reduce(f32[]{:T(128)} %multiply_reduce_fusion.3), channel_id=1, replica_groups=mesh['day'=2,'stu'=16] {'day','stu'}, use_global_device_ids=true, to_apply=%region_8.10 | all-reduce | flops 1 | bytes 8 | tf_op jit(solution)/shard_map/psum | solution.py:61
  418.5 3.2 collective-permute-done.40
  422.5 3.2 collective-permute-done.41
  430.5 3.2 collective-permute-done.43
  441.6 3.4 collective-permute-start.46
  446.4 4.4 collective-permute-start.47
  452.2 4.9 collective-permute-start.48
  457.2 4.5 fusion.78
  461.7 4.3 collective-permute-start.50
  467.3 5.3 multiply_reduce_fusion.2
  472.6 63.7 %psum.53 = f32[]{:T(128)} all-reduce(f32[]{:T(128)} %get-tuple-element.17), channel_id=1, replica_groups=mesh['day'=2,'stu'=16] {'day','stu'}, use_global_device_ids=true, to_apply=%region_10.12 | all-reduce | flops 1 | bytes 8 | tf_op jit(solution)/shard_map/psum | solution.py:61
  538.3 40.3 %psum.54 = f32[]{:T(128)} all-reduce(f32[]{:T(128)} %get-tuple-element.7), channel_id=1, replica_groups=mesh['day'=2,'stu'=16] {'day','stu'}, use_global_device_ids=true, to_apply=%region_12.14 | all-reduce | flops 1 | bytes 8 | tf_op jit(solution)/shard_map/psum | solution.py:61
  603.0 3.2 collective-permute-done.58
  610.9 3.2 collective-permute-done.60
  614.9 3.2 collective-permute-done.61
  622.1 3.4 collective-permute-start.63
  626.8 4.4 collective-permute-start.64
  632.7 4.9 collective-permute-start.65
  637.6 4.5 fusion.46
  642.1 4.3 collective-permute-start.67
  647.8 5.3 multiply_reduce_fusion
  653.0 63.7 %psum.55 = f32[]{:T(128)} all-reduce(f32[]{:T(128)} %get-tuple-element.19), channel_id=1, replica_groups=mesh['day'=2,'stu'=16] {'day','stu'}, use_global_device_ids=true, to_apply=%region_14.16 | all-reduce | flops 1 | bytes 8 | tf_op jit(solution)/shard_map/psum | solution.py:61
  (200 shorter events, 128.4 us)
Async XLA Ops:
  7.2 150.4 %all-reduce.3.cloned.1.call-start = ((), (), s32[]{:S(2)}) async-start(), calls=%async_computation.2 | async-start | bytes 524288 | tf_op jit(solution)/shard_map/psum | solution.py:65
  12.7 4.0 collective-permute-start.2
  16.6 4.0 collective-permute-start.3
  20.6 4.0 collective-permute-start.4
  24.6 4.0 collective-permute-start.5
  28.6 4.0 collective-permute-start.6
  32.5 4.0 collective-permute-start.7
  36.5 4.0 collective-permute-start.8
  40.5 4.0 collective-permute-start.9
  40.6 28.1 %collective-permute-start.15 = (f32[7,16]{0,1:T(8,128)S(1)}, f32[7,16]{0,1:T(8,128)S(1)}, u32[]{:S(2)}, u32[]{:S(2)}) collective-permute-start(f32[7,16]{0,1:T(8,128)S(1)} %slice.333), channel_id=1, source_target_pairs={{0,16},{1,17},{2,18},{3,19},{4,20},{5,21},{6,22},{7,23},{8,24},{9,... | collective-permute-start | bytes 1352 | tf_op jit(solution)/shard_map/ppermute | solution.py:25
  44.5 4.0 collective-permute-start.10
  46.2 169.8 %reduce-scatter.2.cloned.1.call-start = ((), (), s32[]{:S(2)}) async-start(), calls=%async_computation.1 | async-start | bytes 139264 | tf_op jit(solution)/shard_map/reduce_scatter | solution.py:83
  52.4 6.0 collective-permute-start.12
  58.5 5.2 collective-permute-start.13
  63.6 14.8 %collective-permute-start.14 = (f32[32,16]{0,1:T(8,128)S(1)}, f32[32,16]{0,1:T(8,128)S(1)}, u32[]{:S(2)}, u32[]{:S(2)}) collective-permute-start(f32[32,16]{0,1:T(8,128)S(1)} %collective-permute-done.13), channel_id=1, source_target_pairs={{0,15},{1,0},{2,1},{3,2},{4,3},{5,4},{6,5},{7,6},{8,7},{9,8},{10,9... | collective-permute-start | bytes 6152 | tf_op jit(solution)/shard_map/ppermute | solution.py:16
  73.2 85.1 %collective-permute-start.16 = (f32[7,16]{0,1:T(8,128)S(1)}, f32[7,16]{0,1:T(8,128)S(1)}, u32[]{:S(2)}, u32[]{:S(2)}) collective-permute-start(f32[7,16]{0,1:T(8,128)S(1)} %bitcast.23), channel_id=1, source_target_pairs={{16,0},{17,1},{18,2},{19,3},{20,4},{21,5},{22,6},{23,7},{24,8},{25... | collective-permute-start | bytes 1352 | tf_op jit(solution)/shard_map/ppermute | solution.py:25
  232.1 4.0 collective-permute-start.21
  236.0 4.0 collective-permute-start.22
  240.0 4.0 collective-permute-start.23
  244.0 4.0 collective-permute-start.24
  248.0 4.0 collective-permute-start.25
  251.9 4.0 collective-permute-start.26
  255.9 4.0 collective-permute-start.27
  259.9 4.0 collective-permute-start.28
  263.9 4.0 collective-permute-start.29
  267.9 5.0 collective-permute-start.30
  271.5 6.3 collective-permute-start.32
  272.9 14.8 %collective-permute-start.31 = (f32[32,16]{0,1:T(8,128)S(1)}, f32[32,16]{0,1:T(8,128)S(1)}, u32[]{:S(2)}, u32[]{:S(2)}) collective-permute-start(f32[32,16]{0,1:T(8,128)S(1)} %collective-permute-done.30), channel_id=1, source_target_pairs={{0,15},{1,0},{2,1},{3,2},{4,3},{5,4},{6,5},{7,6},{8,7},{9,8},{10,9... | collective-permute-start | bytes 6152 | tf_op jit(solution)/shard_map/ppermute | solution.py:16
  282.3 5.6 collective-permute-start.33
  413.8 4.0 collective-permute-start.39
  417.8 4.0 collective-permute-start.40
  421.8 4.0 collective-permute-start.41
  425.7 4.0 collective-permute-start.42
  429.7 4.0 collective-permute-start.43
  433.7 4.0 collective-permute-start.44
  441.6 4.7 collective-permute-start.46
  446.4 5.8 collective-permute-start.47
  450.9 6.3 collective-permute-start.49
  452.2 14.8 %collective-permute-start.48 = (f32[32,16]{0,1:T(8,128)S(1)}, f32[32,16]{0,1:T(8,128)S(1)}, u32[]{:S(2)}, u32[]{:S(2)}) collective-permute-start(f32[32,16]{0,1:T(8,128)S(1)} %collective-permute-done.47), channel_id=1, source_target_pairs={{0,15},{1,0},{2,1},{3,2},{4,3},{5,4},{6,5},{7,6},{8,7},{9,8},{10,9... | collective-permute-start | bytes 6152 | tf_op jit(solution)/shard_map/ppermute | solution.py:16
  461.7 5.6 collective-permute-start.50
  602.2 4.0 collective-permute-start.58
  610.2 4.0 collective-permute-start.60
  618.1 4.0 collective-permute-start.62
  622.1 4.7 collective-permute-start.63
  626.8 5.8 collective-permute-start.64
  631.3 6.3 collective-permute-start.66
  632.7 14.8 %collective-permute-start.65 = (f32[32,16]{0,1:T(8,128)S(1)}, f32[32,16]{0,1:T(8,128)S(1)}, u32[]{:S(2)}, u32[]{:S(2)}) collective-permute-start(f32[32,16]{0,1:T(8,128)S(1)} %collective-permute-done.64), channel_id=1, source_target_pairs={{0,15},{1,0},{2,1},{3,2},{4,3},{5,4},{6,5},{7,6},{8,7},{9,8},{10,9... | collective-permute-start | bytes 6152 | tf_op jit(solution)/shard_map/ppermute | solution.py:16
  642.1 5.6 collective-permute-start.67
  (26 other events, 198.1 us)
Sparse Core Ops, SparseCore 0:
  46.3 111.2 all-reduce.2
  161.0 54.9 reduce-scatter.1
